TPU v7x, 256 devices: a whole 4x4x8 slice. The times are simulated.
256 devices in a mesh: row: 32 (over y, z), col: 8 (over x, core).
Axes of the slice: x: 4, y: 4, z: 8, core: 2. Of those that a mesh axis runs over, the one named last changes fastest.
Arguments:
- panel_one: bfloat16 [512, 32768], P('col', 'row'), may hold values from -1.1953125 to 1.1953125
- panel_two: bfloat16 [512, 32768], P('col', 'row'), may hold values from -3 to 3
- inverse_one: bfloat16 [512, 512], replicated
- inverse_two: bfloat16 [512, 512], replicated
- column_blocks: int32 [4], replicated, may hold values from 0 to 255, as said below
- row_map: int32 [256], P('row'), may hold values from 0 to 255, as said below
- targets: bfloat16 [32, 8, 128, 128, 128], P('row', 'col'), may hold values from -6 to 6
- rows_one: int32 [32, 8, 128], P('row', 'col'), may hold values from 0 to 255, as said below
- cols_one: int32 [32, 8, 128], P('row', 'col'), may hold values from 0 to 255, as said below
- rows_two: int32 [32, 8, 128], P('row', 'col'), may hold values from 0 to 255, as said below
- cols_two: int32 [32, 8, 128], P('row', 'col'), may hold values from 0 to 255, as said below
Outputs:
- lower_one: bfloat16 [512, 32768], P('col', 'row')
- lower_two: bfloat16 [512, 32768], P('col', 'row')
- trailing: bfloat16 [32, 8, 128, 128, 128], P('row', 'col')
Inputs may be any that keep to these rules, and one draw needn't show every extreme that they name: `column_blocks`: the entries are distinct. row_map[j] // 8 equals j // 8; within each aligned run of 8 entries every value of the run appears once. rows_one[r, c, s] // 8 equals r. cols_one[r, c, s] % 8 equals c. rows_two[r, c, s] // 8 equals r. cols_two[r, c, s] % 8 equals c.
All inputs are finite; a program needn't handle non-finite values.
Results may differ from a plain program's by a relative error of at most 0.006.
Values may be sent and summed in bfloat16 or wider, within the bound.
A program may use at most 192 MiB of HBM per device.

v0:
```python
import jax
import jax.numpy as jnp
from jax import lax
from jax.sharding import PartitionSpec as P


def factor_panel(panel_part, inverse):
    summed = jnp.dot(
        inverse,
        lax.all_gather(panel_part, "col", axis=0, tiled=True),
        preferred_element_type=jnp.float32,
    )
    return summed.astype(jnp.bfloat16)


def bridge_columns(lower_full, column_blocks, slab_rows, block_size):
    local_count = lower_full.shape[1] // block_size
    begin_col = lax.axis_index("col") * slab_rows
    chosen = column_blocks[begin_col // block_size]
    offset = begin_col % block_size
    column_piece = lax.dynamic_slice_in_dim(
        lower_full, chosen % local_count * block_size + offset, slab_rows, 1
    )
    owner_row = chosen // local_count
    owned_here = owner_row == lax.axis_index("row")
    summed = lax.psum(
        jnp.where(owned_here, column_piece.astype(jnp.float32), 0.0).astype(jnp.bfloat16), "row"
    )
    return summed


def pick_tiles(lower_full, block_size):
    col_count = lax.axis_size("col")
    panel_width, row_count = lower_full.shape
    grouped = lower_full.reshape(
        panel_width, row_count // (block_size * col_count), col_count, block_size
    )
    chosen = lax.dynamic_index_in_dim(grouped, lax.axis_index("col"), 2, keepdims=False)
    return chosen.reshape(panel_width, -1)


def gather_tiles(lower_full, block_size):
    return lax.all_gather(pick_tiles(lower_full, block_size), "row", axis=1, tiled=True)


def schur_terms(lower_full, tiles, slot_rows, slot_cols, block_size):
    panel_width = lower_full.shape[0]
    local_blocks = lower_full.reshape(panel_width, -1, block_size)
    column_set = tiles.reshape(panel_width, -1, block_size)
    local_count = local_blocks.shape[1]
    left_tiles = jnp.take(local_blocks, slot_rows.reshape(-1) % local_count, axis=1)
    right_tiles = jnp.take(column_set, slot_cols.reshape(-1) // lax.axis_size("col"), axis=1)
    return jnp.einsum("wsx,wsy->sxy", left_tiles, right_tiles, preferred_element_type=jnp.float32)


def own_slice(lower_full, slab_rows):
    return lax.dynamic_slice_in_dim(lower_full, lax.axis_index("col") * slab_rows, slab_rows, 0)


def per_device(
    panel_one,
    panel_two,
    inverse_one,
    inverse_two,
    column_blocks,
    row_map,
    targets,
    rows_one,
    cols_one,
    rows_two,
    cols_two,
):
    block_size = targets.shape[-1]
    slab_rows = panel_one.shape[0]
    panel_width = inverse_one.shape[0]
    row_count = panel_one.shape[1]
    local_count = row_count // block_size
    lower_one = factor_panel(panel_one, inverse_one)
    blocks_one = lower_one.reshape(panel_width, local_count, block_size)
    bridge = bridge_columns(lower_one, column_blocks, slab_rows, block_size)
    mapped = jnp.take(blocks_one, row_map % local_count, axis=1).reshape(panel_width, row_count)
    update = lax.dot_general(
        bridge, mapped, (((0,), (0,)), ((), ())), preferred_element_type=jnp.float32
    )
    updated = (panel_two.astype(jnp.float32) - update).astype(jnp.bfloat16)
    lower_two = factor_panel(updated, inverse_two)
    tiles_one = gather_tiles(lower_one, block_size)
    tiles_two = gather_tiles(lower_two, block_size)
    terms = schur_terms(lower_one, tiles_one, rows_one, cols_one, block_size)
    terms = terms + schur_terms(lower_two, tiles_two, rows_two, cols_two, block_size)
    trailing = (
        (targets.astype(jnp.float32).reshape(terms.shape) - terms)
        .astype(jnp.bfloat16)
        .reshape(targets.shape)
    )
    return (own_slice(lower_one, slab_rows), own_slice(lower_two, slab_rows), trailing)


def solution(mesh):
    return jax.shard_map(
        per_device,
        mesh=mesh,
        in_specs=(
            P("col", "row"),
            P("col", "row"),
            P(),
            P(),
            P(),
            P("row"),
            P("row", "col", None, None, None),
            P("row", "col", None),
            P("row", "col", None),
            P("row", "col", None),
            P("row", "col", None),
        ),
        out_specs=(P("col", "row"), P("col", "row"), P("row", "col", None, None, None)),
        check_vma=False,
    )
```

profile of v0, /device:TPU:2, one launch (start us, length us, event | category | flops | bytes accessed | tf_op | source)
XLA Modules:
  0.0 418.5 jit_solution(15414585895211025504)
XLA Ops:
  8.0 1.2 dynamic_slice.20
  12.7 24.4 %all-gather.7.cloned.1.call-done = bf16[512,1024]{1,0:T(8,128)(2,1)} async-done(((bf16[64,1024]{1,0:T(8,128)(2,1)}), bf16[512,1024]{1,0:T(8,128)(2,1)}) %all-gather.7.cloned.1.call-update) | async-done | bytes 1048592 | tf_op jit(solution)/shard_map/all_gather | solution.py:10
  37.1 1.9 convolution_convert_fusion.1
  39.2 0.8 select_convert_fusion
  40.1 1.7 gather_fusion
  41.7 2.3 copy.22
  44.0 2.4 bitcast_select_fusion
  46.4 138.7 %all-reduce.2.cloned.1.call-done = bf16[512,64]{1,0:T(8,128)(2,1)} async-done(((bf16[512,64]{1,0:T(8,128)(2,1)}), bf16[512,64]{1,0:T(8,128)(2,1)}) %all-reduce.2.cloned.1.call-update) | async-done | bytes 65552 | tf_op jit(solution)/shard_map/psum | solution.py:26
  185.1 2.4 fusion.23
  187.5 1.3 copy.30
  188.9 1.6 constant_dynamic-slice_fusion.1
  190.7 19.4 %all-gather.9.cloned.1.call-done = bf16[512,1024]{1,0:T(8,128)(2,1)} async-done(((bf16[64,1024]{1,0:T(8,128)(2,1)}), bf16[512,1024]{1,0:T(8,128)(2,1)}) %all-gather.9.cloned.1.call-update) | async-done | bytes 1048592 | tf_op jit(solution)/shard_map/all_gather | solution.py:10
  210.1 2.1 convolution_convert_fusion
  213.1 8.2 %gather_fusion.1 = bf16[128,512,128]{2,1,0:T(8,128)(2,1)} fusion(bf16[512,8,128]{2,0,1:T(8,128)(2,1)S(1)} %copy_bitcast_fusion, s32[1024]{0:T(1024)S(1)} %pad_clamp_fusion.3), kind=kCustom, calls=%fused_computation.clone | custom fusion | bytes 33554944 | tf_op jit(solution)/shard_map/jit(_take)/gather | solution.py:51
  221.3 1.6 constant_dynamic-slice_fusion.2
  223.8 8.2 %gather_fusion.3 = bf16[128,512,128]{1,2,0:T(8,128)(2,1)} fusion(bf16[512,8,128]{0,2,1:T(8,128)(2,1)S(1)} %bitcast.77, s32[1024]{0:T(1024)S(1)} %pad_clamp_fusion.1), kind=kCustom, calls=%fused_computation.2.clone | custom fusion | bytes 33554944 | tf_op jit(solution)/shard_map/jit(_take)/gather | solution.py:51
  232.1 63.8 %all-gather.11.cloned.1.call-done = bf16[512,1,1,4096]{0,3,2,1:T(8,128)(2,1)} async-done(((bf16[512,1,1,128]{0,3,2,1:T(8,128)(2,1)}), bf16[512,1,1,4096]{0,3,2,1:T(8,128)(2,1)}) %all-gather.11.cloned.1.call-update) | async-done | bytes 4194320 | tf_op jit(solution)/shard_map/all_gather | solution.py:43
  295.9 6.4 %copy.25 = bf16[512,32,128]{2,0,1:T(8,128)(2,1)} copy(bf16[512,32,128]{0,2,1:T(8,128)(2,1)} %bitcast.79) | data formatting | bytes 8388608 | tf_op jit(solution)/shard_map/reshape | solution.py:49
  302.3 10.6 %gather_fusion.2 = bf16[128,512,128]{2,1,0:T(8,128)(2,1)} fusion(bf16[512,32,128]{2,0,1:T(8,128)(2,1)} %copy.25, s32[1024]{0:T(1024)S(1)} %pad_clamp_fusion.2), kind=kCustom, calls=%fused_computation.1.clone | custom fusion | bytes 33554944 | tf_op jit(solution)/shard_map/jit(_take)/gather | solution.py:52
  312.9 16.8 %fusion.3 = f32[128,128,128]{2,1,0:T(8,128)} fusion(bf16[128,512,128]{2,1,0:T(8,128)(2,1)} %gather_fusion.2, bf16[128,512,128]{2,1,0:T(8,128)(2,1)} %gather_fusion.1, pred[128]{0:T(512)(128)(4,1)S(1)} %get-tuple-element.20, pred[128]{0:T(512)(128)(4,1)S(1)} %get-tuple-element.26), kind=kOutput, calls=%fused_computation.8 | convolution fusion | flops 2164260864 | bytes 41943296 | tf_op jit(solution)/shard_map/wsx,wsy->sxy/dot_general | solution.py:53
  329.7 47.2 %all-gather.13.cloned.1.call-done = bf16[512,1,1,4096]{0,3,2,1:T(8,128)(2,1)} async-done(((bf16[512,1,1,128]{0,3,2,1:T(8,128)(2,1)}), bf16[512,1,1,4096]{0,3,2,1:T(8,128)(2,1)}) %all-gather.13.cloned.1.call-update) | async-done | bytes 4194320 | tf_op jit(solution)/shard_map/all_gather | solution.py:43
  376.9 6.4 %copy.27 = bf16[512,32,128]{2,0,1:T(8,128)(2,1)} copy(bf16[512,32,128]{0,2,1:T(8,128)(2,1)} %bitcast.80) | data formatting | bytes 8388608 | tf_op jit(solution)/shard_map/reshape | solution.py:49
  383.3 10.5 %gather_fusion.4 = bf16[128,512,128]{2,1,0:T(8,128)(2,1)} fusion(bf16[512,32,128]{2,0,1:T(8,128)(2,1)} %copy.27, s32[1024]{0:T(1024)S(1)} %pad_clamp_fusion), kind=kCustom, calls=%fused_computation.3.clone | custom fusion | bytes 33554944 | tf_op jit(solution)/shard_map/jit(_take)/gather | solution.py:52
  393.8 18.2 %fusion.18 = bf16[1,1,128,128,128]{4,3,2,1,0:T(8,128)(2,1)} fusion(f32[128,128,128]{2,1,0:T(8,128)} %fusion.3, bf16[1,1,128,128,128]{4,3,2,1,0:T(8,128)(2,1)} %param.21, bf16[128,512,128]{2,1,0:T(8,128)(2,1)} %gather_fusion.4, pred[128]{0:T(512)(128)(4,1)S(1)} %get-tuple-element.16, bf16[128,512,128]{1,2,0:T(8,128)(2,1)} %gather_fusion.3, ...), kind=kOutput, calls=%fused_computation.24 | convolution fusion | flops 2172649472 | bytes 50331904 | tf_op jit(solution)/shard_map/wsx,wsy->sxy/dot_general | solution.py:53
  (37 shorter events, 3.7 us)
Async XLA Ops:
  7.2 29.9 %copy-start = (bf16[512,512]{1,0:T(8,128)(2,1)S(1)}, bf16[512,512]{1,0:T(8,128)(2,1)}, u32[]{:S(2)}) copy-start(bf16[512,512]{1,0:T(8,128)(2,1)} %param.17) | copy-start | bytes 1572868
  7.2 205.8 %copy-start.3 = (s32[1,1,128]{2,1,0:T(1,128)S(1)}, s32[1,1,128]{2,1,0:T(1,128)}, u32[]{:S(2)}) copy-start(s32[1,1,128]{2,1,0:T(1,128)} %param.23) | copy-start | bytes 1540
  7.2 205.8 %copy-start.4 = (s32[1,1,128]{2,1,0:T(1,128)S(1)}, s32[1,1,128]{2,1,0:T(1,128)}, u32[]{:S(2)}) copy-start(s32[1,1,128]{2,1,0:T(1,128)} %param.22) | copy-start | bytes 1540
  7.2 205.8 %copy-start.5 = (s32[1,1,128]{2,1,0:T(1,128)S(1)}, s32[1,1,128]{2,1,0:T(1,128)}, u32[]{:S(2)}) copy-start(s32[1,1,128]{2,1,0:T(1,128)} %param.25) | copy-start | bytes 1540
  7.2 205.8 %copy-start.6 = (s32[1,1,128]{2,1,0:T(1,128)S(1)}, s32[1,1,128]{2,1,0:T(1,128)}, u32[]{:S(2)}) copy-start(s32[1,1,128]{2,1,0:T(1,128)} %param.24) | copy-start | bytes 1540
  7.2 29.8 %all-gather.7.cloned.1.call-start = ((), (), s32[]{:S(2)}) async-start(), calls=%async_computation | async-start | bytes 1179648 | tf_op jit(solution)/shard_map/all_gather | solution.py:10
  8.0 177.1 %all-reduce.2.cloned.1.call-start = ((), (), s32[]{:S(2)}) async-start(), calls=%async_computation.1 | async-start | bytes 262144 | tf_op jit(solution)/shard_map/psum | solution.py:26
  39.0 151.7 %copy-start.2 = (bf16[512,1024]{1,0:T(8,128)(2,1)}, bf16[512,1024]{1,0:T(8,128)(2,1)S(1)}, u32[]{:S(2)}) copy-start(bf16[512,1024]{1,0:T(8,128)(2,1)S(1)} %convolution_convert_fusion.1) | copy-start | bytes 3145732
  40.0 170.1 %all-gather.9.cloned.1.call-start = ((), (), s32[]{:S(2)}) async-start(), calls=%async_computation.2 | async-start | bytes 1179648 | tf_op jit(solution)/shard_map/all_gather | solution.py:10
  187.5 108.4 %all-gather.11.cloned.1.call-start = ((), (), s32[]{:S(2)}) async-start(), calls=%async_computation.3 | async-start | bytes 4325376 | tf_op jit(solution)/shard_map/all_gather | solution.py:43
  190.5 186.4 %all-gather.13.cloned.1.call-start = ((), (), s32[]{:S(2)}) async-start(), calls=%async_computation.4 | async-start | bytes 4325376 | tf_op jit(solution)/shard_map/all_gather | solution.py:43
  393.8 18.2 %copy-start.1 = (bf16[512,512]{1,0:T(8,128)(2,1)S(1)}, bf16[512,512]{1,0:T(8,128)(2,1)}, u32[]{:S(2)}) copy-start(bf16[512,512]{1,0:T(8,128)(2,1)} %param.17) | copy-start | bytes 1572868
Sparse Core Ops, SparseCore 0:
  9.9 27.1 all-gather.6
  41.1 143.9 all-reduce.1
  187.6 22.4 all-gather.8
  212.6 83.2 all-gather.10
  298.3 78.5 all-gather.12
where the time goes:
time: 419 us
  waiting for transfers between devices  294 us (70%)
  local copies, waits for them, and re-layouts  61.9 us (15%)
  matrix products  41.4 us (10%)
  between operations  16.6 us (4%)
    psum x1, waiting for transfers between devices, bridge_columns(): lax.psum(jnp.where(owned_here, column_piece.astype(jnp.float32), 0.0).ast...  139 us
    all_gather x2, waiting for transfers between devices, gather_tiles(): lax.all_gather(pick_tiles(lower_full, block_size), 'row', axis=1, tiled=T...  111 us
    all_gather x2, waiting for transfers between devices, factor_panel(): lax.all_gather(panel_part, 'col', axis=0, tiled=True)  43.8 us
    dot_general x2, matrix products, schur_terms(): jnp.einsum('wsx,wsy->sxy', left_tiles, right_tiles, preferred_element_typ...  35 us
    gather x2, local copies, waits for them, and re-layouts, schur_terms(): jnp.take(column_set, slot_cols.reshape(-1) // lax.axis_size('col'), axis=1)  21.1 us
    gather x2, local copies, waits for them, and re-layouts, schur_terms(): jnp.take(local_blocks, slot_rows.reshape(-1) % local_count, axis=1)  16.5 us
    reshape x2, local copies, waits for them, and re-layouts, schur_terms(): column_set = tiles.reshape(panel_width, -1, block_size)  12.8 us
  transfers between devices with their start and end apart: 5, of which 5 were waited for; matrix products, arithmetic and copies ran while one was open for 16% of the time, Pallas kernels for 0%

commit v1 on v0

--- a/solution.py
+++ b/solution.py
@@ -2,6 +2,7 @@
 import jax.numpy as jnp
 from jax import lax
 from jax.sharding import PartitionSpec as P
+from jax.lax import all_gather
 
 
 def factor_panel(panel_part, inverse):
@@ -14,6 +15,11 @@
 
 
 def bridge_columns(lower_full, column_blocks, slab_rows, block_size):
+
+    def pipes_supply_all(u):
+        r1 = jnp.sum(all_gather(u, axis_name="row"), axis=0)
+        return r1
+
     local_count = lower_full.shape[1] // block_size
     begin_col = lax.axis_index("col") * slab_rows
     chosen = column_blocks[begin_col // block_size]
@@ -23,8 +29,8 @@
     )
     owner_row = chosen // local_count
     owned_here = owner_row == lax.axis_index("row")
-    summed = lax.psum(
-        jnp.where(owned_here, column_piece.astype(jnp.float32), 0.0).astype(jnp.bfloat16), "row"
+    summed = pipes_supply_all(
+        jnp.where(owned_here, column_piece.astype(jnp.float32), 0.0).astype(jnp.bfloat16)
     )
     return summed
 

time: 419 us -> 359 us (0.86)
  waiting for transfers between devices: 294 us -> 231 us
    psum x1 -> x0, waiting for transfers between devices: 139 us -> none  [bridge_columns(): lax.psum(jnp.where(owned_here, column_piece.astype(jnp.float32), 0.0).ast...]
    all_gather x0 -> x1, waiting for transfers between devices: none -> 76.2 us  [pipes_supply_all(): r1 = jnp.sum(all_gather(u, axis_name='row'), axis=0)]
  transfers between devices with their start and end apart: 5 -> 5, of which waited for: 5 -> 5; matrix products, arithmetic and copies ran while one was open for 16% -> 19% of each run, Pallas kernels for 0% -> 0%
where the time goes in v1:
time: 359 us; the launch traced here: 358 us
  waiting for transfers between devices  231 us (64%)
  local copies, waits for them, and re-layouts  61.9 us (17%)
  matrix products  41.3 us (12%)
  between operations  16.6 us (5%)
  other arithmetic  7.06 us (2%)
    all_gather x2, waiting for transfers between devices, gather_tiles(): lax.all_gather(pick_tiles(lower_full, block_size), 'row', axis=1, tiled=T...  111 us
    all_gather x1, waiting for transfers between devices, pipes_supply_all(): r1 = jnp.sum(all_gather(u, axis_name='row'), axis=0)  76.2 us
    all_gather x2, waiting for transfers between devices, factor_panel(): lax.all_gather(panel_part, 'col', axis=0, tiled=True)  43.1 us
    dot_general x2, matrix products, schur_terms(): jnp.einsum('wsx,wsy->sxy', left_tiles, right_tiles, preferred_element_typ...  35 us
    gather x2, local copies, waits for them, and re-layouts, schur_terms(): jnp.take(column_set, slot_cols.reshape(-1) // lax.axis_size('col'), axis=1)  21.1 us
    gather x2, local copies, waits for them, and re-layouts, schur_terms(): jnp.take(local_blocks, slot_rows.reshape(-1) % local_count, axis=1)  16.5 us
    reshape x2, local copies, waits for them, and re-layouts, schur_terms(): column_set = tiles.reshape(panel_width, -1, block_size)  12.8 us
  transfers between devices with their start and end apart: 5, of which 5 were waited for; matrix products, arithmetic and copies ran while one was open for 19% of the time, Pallas kernels for 0%

profile of v1, /device:TPU:2, one launch (start us, length us, event | category | flops | bytes accessed | tf_op | source)
XLA Modules:
  0.0 358.4 jit_solution(6116448207912589067)
XLA Ops:
  8.0 1.2 dynamic_slice.20
  11.9 25.2 %all-gather.9.cloned.1.call-done = bf16[512,1024]{1,0:T(8,128)(2,1)} async-done(((bf16[64,1024]{1,0:T(8,128)(2,1)}), bf16[512,1024]{1,0:T(8,128)(2,1)}) %all-gather.9.cloned.1.call-update) | async-done | bytes 1048592 | tf_op jit(solution)/shard_map/all_gather | solution.py:11
  37.1 1.9 convolution_convert_fusion.1
  41.0 1.7 gather_fusion
  42.6 2.3 copy.22
  44.9 2.4 bitcast_select_fusion
  47.3 76.2 %all-gather.13.cloned.1.call-done = bf16[16384,64]{1,0:T(8,128)(2,1)} async-done(((bf16[512,64]{1,0:T(8,128)(2,1)}), bf16[16384,64]{1,0:T(8,128)(2,1)}) %all-gather.13.cloned.1.call-update) | async-done | bytes 2097168 | tf_op jit(solution)/shard_map/all_gather | solution.py:20
  123.5 3.0 reduce_sum.12
  126.5 2.3 fusion.23
  129.0 1.3 copy.30
  130.3 1.6 constant_dynamic-slice_fusion.1
  132.1 17.9 %all-gather.11.cloned.1.call-done = bf16[512,1024]{1,0:T(8,128)(2,1)} async-done(((bf16[64,1024]{1,0:T(8,128)(2,1)}), bf16[512,1024]{1,0:T(8,128)(2,1)}) %all-gather.11.cloned.1.call-update) | async-done | bytes 1048592 | tf_op jit(solution)/shard_map/all_gather | solution.py:11
  150.0 2.0 convolution_convert_fusion
  152.8 8.2 %gather_fusion.1 = bf16[128,512,128]{2,1,0:T(8,128)(2,1)} fusion(bf16[512,8,128]{2,0,1:T(8,128)(2,1)S(1)} %copy_bitcast_fusion, s32[1024]{0:T(1024)S(1)} %pad_clamp_fusion.3), kind=kCustom, calls=%fused_computation.clone | custom fusion | bytes 33554944 | tf_op jit(solution)/shard_map/jit(_take)/gather | solution.py:57
  161.1 1.6 constant_dynamic-slice_fusion.2
  163.6 8.2 %gather_fusion.3 = bf16[128,512,128]{1,2,0:T(8,128)(2,1)} fusion(bf16[512,8,128]{0,2,1:T(8,128)(2,1)S(1)} %bitcast.78, s32[1024]{0:T(1024)S(1)} %pad_clamp_fusion.1), kind=kCustom, calls=%fused_computation.2.clone | custom fusion | bytes 33554944 | tf_op jit(solution)/shard_map/jit(_take)/gather | solution.py:57
  171.8 64.0 %all-gather.15.cloned.1.call-done = bf16[512,1,1,4096]{0,3,2,1:T(8,128)(2,1)} async-done(((bf16[512,1,1,128]{0,3,2,1:T(8,128)(2,1)}), bf16[512,1,1,4096]{0,3,2,1:T(8,128)(2,1)}) %all-gather.15.cloned.1.call-update) | async-done | bytes 4194320 | tf_op jit(solution)/shard_map/all_gather | solution.py:49
  235.8 6.4 %copy.25 = bf16[512,32,128]{2,0,1:T(8,128)(2,1)} copy(bf16[512,32,128]{0,2,1:T(8,128)(2,1)} %bitcast.80) | data formatting | bytes 8388608 | tf_op jit(solution)/shard_map/reshape | solution.py:55
  242.2 10.6 %gather_fusion.2 = bf16[128,512,128]{2,1,0:T(8,128)(2,1)} fusion(bf16[512,32,128]{2,0,1:T(8,128)(2,1)} %copy.25, s32[1024]{0:T(1024)S(1)} %pad_clamp_fusion.2), kind=kCustom, calls=%fused_computation.1.clone | custom fusion | bytes 33554944 | tf_op jit(solution)/shard_map/jit(_take)/gather | solution.py:58
  252.8 16.8 %fusion.3 = f32[128,128,128]{2,1,0:T(8,128)} fusion(bf16[128,512,128]{2,1,0:T(8,128)(2,1)} %gather_fusion.2, bf16[128,512,128]{2,1,0:T(8,128)(2,1)} %gather_fusion.1, pred[128]{0:T(512)(128)(4,1)S(1)} %get-tuple-element.20, pred[128]{0:T(512)(128)(4,1)S(1)} %get-tuple-element.26), kind=kOutput, calls=%fused_computation.8 | convolution fusion | flops 2164260864 | bytes 41943296 | tf_op jit(solution)/shard_map/wsx,wsy->sxy/dot_general | solution.py:59
  269.6 47.2 %all-gather.17.cloned.1.call-done = bf16[512,1,1,4096]{0,3,2,1:T(8,128)(2,1)} async-done(((bf16[512,1,1,128]{0,3,2,1:T(8,128)(2,1)}), bf16[512,1,1,4096]{0,3,2,1:T(8,128)(2,1)}) %all-gather.17.cloned.1.call-update) | async-done | bytes 4194320 | tf_op jit(solution)/shard_map/all_gather | solution.py:49
  316.8 6.4 %copy.27 = bf16[512,32,128]{2,0,1:T(8,128)(2,1)} copy(bf16[512,32,128]{0,2,1:T(8,128)(2,1)} %bitcast.81) | data formatting | bytes 8388608 | tf_op jit(solution)/shard_map/reshape | solution.py:55
  323.2 10.5 %gather_fusion.4 = bf16[128,512,128]{2,1,0:T(8,128)(2,1)} fusion(bf16[512,32,128]{2,0,1:T(8,128)(2,1)} %copy.27, s32[1024]{0:T(1024)S(1)} %pad_clamp_fusion), kind=kCustom, calls=%fused_computation.3.clone | custom fusion | bytes 33554944 | tf_op jit(solution)/shard_map/jit(_take)/gather | solution.py:58
  333.7 18.2 %fusion.18 = bf16[1,1,128,128,128]{4,3,2,1,0:T(8,128)(2,1)} fusion(f32[128,128,128]{2,1,0:T(8,128)} %fusion.3, bf16[1,1,128,128,128]{4,3,2,1,0:T(8,128)(2,1)} %param.21, bf16[128,512,128]{2,1,0:T(8,128)(2,1)} %gather_fusion.4, pred[128]{0:T(512)(128)(4,1)S(1)} %get-tuple-element.16, bf16[128,512,128]{1,2,0:T(8,128)(2,1)} %gather_fusion.3, ...), kind=kOutput, calls=%fused_computation.24 | convolution fusion | flops 2172649472 | bytes 50331904 | tf_op jit(solution)/shard_map/wsx,wsy->sxy/dot_general | solution.py:59
  (40 shorter events, 4.6 us)
Async XLA Ops:
  7.2 29.9 %copy-start = (bf16[512,512]{1,0:T(8,128)(2,1)S(1)}, bf16[512,512]{1,0:T(8,128)(2,1)}, u32[]{:S(2)}) copy-start(bf16[512,512]{1,0:T(8,128)(2,1)} %param.17) | copy-start | bytes 1572868
  7.2 142.8 %copy-start.7 = (bf16[512,512]{1,0:T(8,128)(2,1)S(1)}, bf16[512,512]{1,0:T(8,128)(2,1)}, u32[]{:S(2)}) copy-start(bf16[512,512]{1,0:T(8,128)(2,1)} %param.18) | copy-start | bytes 1572868
  7.2 145.5 %copy-start.3 = (s32[1,1,128]{2,1,0:T(1,128)S(1)}, s32[1,1,128]{2,1,0:T(1,128)}, u32[]{:S(2)}) copy-start(s32[1,1,128]{2,1,0:T(1,128)} %param.23) | copy-start | bytes 1540
  7.2 145.5 %copy-start.4 = (s32[1,1,128]{2,1,0:T(1,128)S(1)}, s32[1,1,128]{2,1,0:T(1,128)}, u32[]{:S(2)}) copy-start(s32[1,1,128]{2,1,0:T(1,128)} %param.22) | copy-start | bytes 1540
  7.2 145.6 %copy-start.5 = (s32[1,1,128]{2,1,0:T(1,128)S(1)}, s32[1,1,128]{2,1,0:T(1,128)}, u32[]{:S(2)}) copy-start(s32[1,1,128]{2,1,0:T(1,128)} %param.25) | copy-start | bytes 1540
  7.2 145.6 %copy-start.6 = (s32[1,1,128]{2,1,0:T(1,128)S(1)}, s32[1,1,128]{2,1,0:T(1,128)}, u32[]{:S(2)}) copy-start(s32[1,1,128]{2,1,0:T(1,128)} %param.24) | copy-start | bytes 1540
  7.2 29.8 %all-gather.9.cloned.1.call-start = ((), (), s32[]{:S(2)}) async-start(), calls=%async_computation | async-start | bytes 1179648 | tf_op jit(solution)/shard_map/all_gather | solution.py:11
  8.0 115.6 %all-gather.13.cloned.1.call-start = ((), (), s32[]{:S(2)}) async-start(), calls=%async_computation.2 | async-start | bytes 4325376 | tf_op jit(solution)/shard_map/all_gather | solution.py:20
  39.0 93.1 %copy-start.2 = (bf16[512,1024]{1,0:T(8,128)(2,1)}, bf16[512,1024]{1,0:T(8,128)(2,1)S(1)}, u32[]{:S(2)}) copy-start(bf16[512,1024]{1,0:T(8,128)(2,1)S(1)} %convolution_convert_fusion.1) | copy-start | bytes 3145732
  40.0 110.1 %all-gather.11.cloned.1.call-start = ((), (), s32[]{:S(2)}) async-start(), calls=%async_computation.1 | async-start | bytes 1179648 | tf_op jit(solution)/shard_map/all_gather | solution.py:11
  128.9 106.9 %all-gather.15.cloned.1.call-start = ((), (), s32[]{:S(2)}) async-start(), calls=%async_computation.3 | async-start | bytes 4325376 | tf_op jit(solution)/shard_map/all_gather | solution.py:49
  131.9 184.9 %all-gather.17.cloned.1.call-start = ((), (), s32[]{:S(2)}) async-start(), calls=%async_computation.4 | async-start | bytes 4325376 | tf_op jit(solution)/shard_map/all_gather | solution.py:49
  333.7 18.2 %copy-start.1 = (bf16[512,512]{1,0:T(8,128)(2,1)S(1)}, bf16[512,512]{1,0:T(8,128)(2,1)}, u32[]{:S(2)}) copy-start(bf16[512,512]{1,0:T(8,128)(2,1)} %param.17) | copy-start | bytes 1572868
Sparse Core Ops, SparseCore 0:
  9.9 27.1 all-gather.8
  40.2 83.2 all-gather.12
  129.0 20.9 all-gather.10
  152.5 83.2 all-gather.14
  238.2 78.5 all-gather.16
